TPU v7x, 512 devices: a whole 4x8x8 slice. The times are simulated.
512 devices in a mesh: chain: 8 (over x, core), tile: 64 (over y, z).
Axes of the slice: x: 4, y: 8, z: 8, core: 2. Of those that a mesh axis runs over, the one named last changes fastest.
Arguments:
- right_side: float32 [3, 2, 32, 32768], P(None, None, None, ('chain', 'tile')), may hold values from -6 to 6
- diag_inverse: float32 [2, 32768, 4096], P(None, ('chain', 'tile'))
- coupling: float32 [2, 32768, 4096], P(None, ('chain', 'tile')), may hold values from -0.0390625 to 0.0390625
- updates: float32 [131072, 192], P(('chain', 'tile')), may hold values from -2.4 to 2.4
- update_rows: int32 [131072], P(('chain', 'tile')), may hold values from 0 to 4095, as said below
- tile_counts: int32 [1024], P(('chain', 'tile')), may hold values from 32 to 128, as said below
Outputs:
- solution: float32 [3, 2, 32, 32768], P(None, None, None, ('chain', 'tile'))
Inputs may be any that keep to these rules, and one draw needn't show every extreme that they name: `update_rows`: rows are counted within the supernode of the group that holds the entry. In each aligned block of 256 entries (the update rows of one device) at most 8 entries fall in any one aligned range of 64 rows, and in each run of 64 aligned blocks one such range receives exactly 8 entries from every block of the run. Padding rows carry entries too. `tile_counts`: one tile has all 128 rows live.
All inputs are finite; a program needn't handle non-finite values.
Results may differ from a plain program's by a relative error of at most 0.0001.
Values sent between devices are 32-bit elements; how exact they have to be, the bound alone decides.
A program may use at most 64 MiB of HBM per device.

v0:
```python
import jax
import jax.numpy as jnp
from jax import lax
from jax.sharding import PartitionSpec as P

highest = lax.Precision.HIGHEST


def shifted(value, axis, by):
    peers = lax.axis_size(axis)
    pairs = [(i, i + by) for i in range(peers) if 0 <= i + by < peers]
    return lax.ppermute(value, axis, pairs)


def combine_parts(products):
    return jnp.stack([products[0, 0] - products[1, 1], products[0, 1] + products[1, 0]], axis=0)


def body(right_side, diag_inverse, coupling, updates, update_rows, tile_counts):
    batches, halves, sources, own_rows = right_side.shape
    chain_size = lax.axis_size("chain")
    full_rows = diag_inverse.shape[2]
    row_count = updates.shape[0]
    tile_rows = row_count // tile_counts.shape[0]
    limits = jnp.broadcast_to(tile_counts[:, None], (tile_counts.shape[0], tile_rows)).reshape(-1)
    is_live = jnp.arange(row_count, dtype=jnp.int32) % tile_rows < limits
    live_updates = jnp.where(is_live[:, None], updates, 0.0)
    dense_sum = jax.ops.segment_sum(live_updates, update_rows, num_segments=full_rows)
    accumulated = lax.psum_scatter(dense_sum, "tile", scatter_dimension=0, tiled=True)
    arranged = accumulated.reshape(own_rows, batches, halves, sources).transpose(1, 2, 3, 0)
    reduced_all = right_side - arranged
    chain_index = lax.axis_index("chain")
    section_count = chain_size + batches - 1

    def accumulate(columns):
        diag_part = jnp.einsum("jrs,kis->kjri", columns, diag_inverse, precision=highest)
        couple_part = jnp.einsum("jrs,kis->kjri", columns, coupling, precision=highest)
        return (diag_part, couple_part)

    def advance(section_index, loop_state):
        carried, solution = loop_state
        incoming = shifted(carried, "chain", 1)
        batch_index = section_index - chain_index
        active = (batch_index >= 0) & (batch_index < batches)
        clamped = jnp.clip(batch_index, 0, batches - 1)
        reduced = lax.dynamic_index_in_dim(reduced_all, clamped, 0, keepdims=False) - incoming
        diag_sum, couple_sum = accumulate(lax.all_gather(reduced, "tile", axis=2, tiled=True))
        updated = lax.dynamic_update_index_in_dim(solution, combine_parts(diag_sum), clamped, 0)
        return (combine_parts(couple_sum), jnp.where(active, updated, solution))

    start_state = (jnp.zeros((2, sources, own_rows), jnp.float32), jnp.zeros_like(right_side))
    final_carry, solution = lax.fori_loop(0, section_count, advance, start_state)
    return solution


def solution(mesh):
    in_specs = (
        P(None, None, None, ("chain", "tile")),
        P(None, ("chain", "tile"), None),
        P(None, ("chain", "tile"), None),
        P(("chain", "tile"), None),
        P(("chain", "tile")),
        P(("chain", "tile")),
    )
    out_specs = P(None, None, None, ("chain", "tile"))
    return jax.shard_map(body, mesh=mesh, in_specs=in_specs, out_specs=out_specs, check_vma=False)
```

profile of v0, /device:TPU:2, one launch (start us, length us, event | category | flops | bytes accessed | tf_op | source)
XLA Modules:
  0.0 1293.3 jit_solution(14064460779872113943)
XLA Ops:
  7.3 0.9 broadcast_select_fusion
  8.3 4.2 scatter_custom_fusion
  12.6 251.8 %reduce-scatter.2.cloned.1.call-done = f32[64,192]{1,0:T(8,128)} async-done(((f32[4096,192]{1,0:T(8,128)}), f32[64,192]{1,0:T(8,128)}) %reduce-scatter.2.cloned.1.call-update) | async-done | bytes 49168 | tf_op jit(solution)/shard_map/reduce_scatter | solution.py:29
  265.4 1020.7 %while.15 = (s32[]{:T(128)}, f32[2,32,64]{2,1,0:T(8,128)S(1)}, f32[3,2,32,64]{3,2,1,0:T(8,128)S(1)}, s32[]{:T(128)}, f32[3,2,32,64]{3,2,1,0:T(8,128)S(1)}, /*ind...) while((s32[]{:T(128)}, f32[2,32,64]{2,1,0:T(8,128)S(1)}, ...), condition=%wide.region_3.4_spmd, body=%wide.region_2.3_spmd.sunk | while | flops 805330944 | bytes 23675160 | solution.py:52
  265.6 1.9 collective-permute-start
  267.6 3.5 collective-permute-done
  271.9 84.3 %all-gather.2.cloned.1.call-done = f32[2,32,4096]{1,0,2:T(2,128)} async-done(((f32[2,32,64]{1,0,2:T(2,128)}), f32[2,32,4096]{1,0,2:T(2,128)}) %all-gather.2.cloned.1.call-update) | async-done | bytes 1048592 | tf_op jit(solution)/shard_map/while/body/eval_jaxpr/all_gather | solution.py:47
  356.2 5.2 copy.48
  361.4 3.1 fusion.38
  364.6 3.1 fusion.41
  368.0 1.9 collective-permute-start
  370.0 3.5 collective-permute-done
  374.2 84.0 %all-gather.2.cloned.1.call-done = f32[2,32,4096]{1,0,2:T(2,128)} async-done(((f32[2,32,64]{1,0,2:T(2,128)}), f32[2,32,4096]{1,0,2:T(2,128)}) %all-gather.2.cloned.1.call-update) | async-done | bytes 1048592 | tf_op jit(solution)/shard_map/while/body/eval_jaxpr/all_gather | solution.py:47
  458.2 5.2 copy.48
  463.5 3.1 fusion.38
  466.6 3.1 fusion.41
  470.0 1.9 collective-permute-start
  472.0 3.5 collective-permute-done
  476.3 84.0 %all-gather.2.cloned.1.call-done = f32[2,32,4096]{1,0,2:T(2,128)} async-done(((f32[2,32,64]{1,0,2:T(2,128)}), f32[2,32,4096]{1,0,2:T(2,128)}) %all-gather.2.cloned.1.call-update) | async-done | bytes 1048592 | tf_op jit(solution)/shard_map/while/body/eval_jaxpr/all_gather | solution.py:47
  560.3 5.2 copy.48
  565.5 3.1 fusion.38
  568.7 3.1 fusion.41
  572.0 1.9 collective-permute-start
  574.1 3.5 collective-permute-done
  578.3 84.0 %all-gather.2.cloned.1.call-done = f32[2,32,4096]{1,0,2:T(2,128)} async-done(((f32[2,32,64]{1,0,2:T(2,128)}), f32[2,32,4096]{1,0,2:T(2,128)}) %all-gather.2.cloned.1.call-update) | async-done | bytes 1048592 | tf_op jit(solution)/shard_map/while/body/eval_jaxpr/all_gather | solution.py:47
  662.3 5.2 copy.48
  667.6 3.1 fusion.38
  670.7 3.1 fusion.41
  674.1 1.9 collective-permute-start
  676.1 3.5 collective-permute-done
  680.4 84.0 %all-gather.2.cloned.1.call-done = f32[2,32,4096]{1,0,2:T(2,128)} async-done(((f32[2,32,64]{1,0,2:T(2,128)}), f32[2,32,4096]{1,0,2:T(2,128)}) %all-gather.2.cloned.1.call-update) | async-done | bytes 1048592 | tf_op jit(solution)/shard_map/while/body/eval_jaxpr/all_gather | solution.py:47
  764.4 5.2 copy.48
  769.6 3.1 fusion.38
  772.8 3.1 fusion.41
  776.1 1.9 collective-permute-start
  778.2 3.5 collective-permute-done
  782.4 84.0 %all-gather.2.cloned.1.call-done = f32[2,32,4096]{1,0,2:T(2,128)} async-done(((f32[2,32,64]{1,0,2:T(2,128)}), f32[2,32,4096]{1,0,2:T(2,128)}) %all-gather.2.cloned.1.call-update) | async-done | bytes 1048592 | tf_op jit(solution)/shard_map/while/body/eval_jaxpr/all_gather | solution.py:47
  866.4 5.2 copy.48
  871.6 3.1 fusion.38
  874.8 3.1 fusion.41
  878.2 1.9 collective-permute-start
  880.2 3.5 collective-permute-done
  884.4 84.0 %all-gather.2.cloned.1.call-done = f32[2,32,4096]{1,0,2:T(2,128)} async-done(((f32[2,32,64]{1,0,2:T(2,128)}), f32[2,32,4096]{1,0,2:T(2,128)}) %all-gather.2.cloned.1.call-update) | async-done | bytes 1048592 | tf_op jit(solution)/shard_map/while/body/eval_jaxpr/all_gather | solution.py:47
  968.4 5.2 copy.48
  973.7 3.1 fusion.38
  976.8 3.1 fusion.41
  980.2 1.9 collective-permute-start
  982.2 3.5 collective-permute-done
  986.5 84.0 %all-gather.2.cloned.1.call-done = f32[2,32,4096]{1,0,2:T(2,128)} async-done(((f32[2,32,64]{1,0,2:T(2,128)}), f32[2,32,4096]{1,0,2:T(2,128)}) %all-gather.2.cloned.1.call-update) | async-done | bytes 1048592 | tf_op jit(solution)/shard_map/while/body/eval_jaxpr/all_gather | solution.py:47
  1070.5 5.2 copy.48
  1075.7 3.1 fusion.38
  1078.9 3.1 fusion.41
  1082.2 1.9 collective-permute-start
  1084.3 3.5 collective-permute-done
  1088.5 84.0 %all-gather.2.cloned.1.call-done = f32[2,32,4096]{1,0,2:T(2,128)} async-done(((f32[2,32,64]{1,0,2:T(2,128)}), f32[2,32,4096]{1,0,2:T(2,128)}) %all-gather.2.cloned.1.call-update) | async-done | bytes 1048592 | tf_op jit(solution)/shard_map/while/body/eval_jaxpr/all_gather | solution.py:47
  1172.5 5.2 copy.48
  1177.8 3.1 fusion.38
  1180.9 3.1 fusion.41
  1184.3 1.9 collective-permute-start
  1186.3 3.5 collective-permute-done
  1190.5 84.0 %all-gather.2.cloned.1.call-done = f32[2,32,4096]{1,0,2:T(2,128)} async-done(((f32[2,32,64]{1,0,2:T(2,128)}), f32[2,32,4096]{1,0,2:T(2,128)}) %all-gather.2.cloned.1.call-update) | async-done | bytes 1048592 | tf_op jit(solution)/shard_map/while/body/eval_jaxpr/all_gather | solution.py:47
  1274.5 5.2 copy.48
  1279.8 3.1 fusion.38
  1283.0 3.1 fusion.41
  (154 shorter events, 12.2 us)
Async XLA Ops:
  6.5 257.9 %reduce-scatter.2.cloned.1.call-start = ((), (), s32[]{:S(2)}) async-start(), calls=%async_computation.1 | async-start | bytes 4259840 | tf_op jit(solution)/shard_map/reduce_scatter | solution.py:29
  12.6 252.8 %copy-start.3 = (f32[3,2,32,64]{3,2,1,0:T(8,128)S(1)}, f32[3,2,32,64]{3,2,1,0:T(8,128)}, u32[]{:S(2)}) copy-start(f32[3,2,32,64]{3,2,1,0:T(8,128)} %param.8) | copy-start | bytes 147460
  12.6 252.8 %copy-start = (f32[2,64,4096]{2,1,0:T(8,128)S(1)}, f32[2,64,4096]{2,1,0:T(8,128)}, u32[]{:S(2)}) copy-start(f32[2,64,4096]{2,1,0:T(8,128)} %param.10) | copy-start | bytes 6291460
  265.4 90.8 %all-gather.2.cloned.1.call-start = ((), (), s32[]{:S(2)}) async-start(), calls=%async_computation.2 | async-start | bytes 4259840 | tf_op jit(solution)/shard_map/while/body/eval_jaxpr/all_gather | solution.py:47
  265.6 5.6 collective-permute-start
  361.4 3.2 copy-start.1
  367.8 90.4 %all-gather.2.cloned.1.call-start = ((), (), s32[]{:S(2)}) async-start(), calls=%async_computation.2 | async-start | bytes 4259840 | tf_op jit(solution)/shard_map/while/body/eval_jaxpr/all_gather | solution.py:47
  368.0 5.6 collective-permute-start
  463.5 3.2 copy-start.1
  469.9 90.4 %all-gather.2.cloned.1.call-start = ((), (), s32[]{:S(2)}) async-start(), calls=%async_computation.2 | async-start | bytes 4259840 | tf_op jit(solution)/shard_map/while/body/eval_jaxpr/all_gather | solution.py:47
  470.0 5.6 collective-permute-start
  565.5 3.2 copy-start.1
  571.9 90.4 %all-gather.2.cloned.1.call-start = ((), (), s32[]{:S(2)}) async-start(), calls=%async_computation.2 | async-start | bytes 4259840 | tf_op jit(solution)/shard_map/while/body/eval_jaxpr/all_gather | solution.py:47
  572.0 5.6 collective-permute-start
  667.6 3.2 copy-start.1
  673.9 90.4 %all-gather.2.cloned.1.call-start = ((), (), s32[]{:S(2)}) async-start(), calls=%async_computation.2 | async-start | bytes 4259840 | tf_op jit(solution)/shard_map/while/body/eval_jaxpr/all_gather | solution.py:47
  674.1 5.6 collective-permute-start
  769.6 3.2 copy-start.1
  776.0 90.4 %all-gather.2.cloned.1.call-start = ((), (), s32[]{:S(2)}) async-start(), calls=%async_computation.2 | async-start | bytes 4259840 | tf_op jit(solution)/shard_map/while/body/eval_jaxpr/all_gather | solution.py:47
  776.1 5.6 collective-permute-start
  871.6 3.2 copy-start.1
  878.0 90.4 %all-gather.2.cloned.1.call-start = ((), (), s32[]{:S(2)}) async-start(), calls=%async_computation.2 | async-start | bytes 4259840 | tf_op jit(solution)/shard_map/while/body/eval_jaxpr/all_gather | solution.py:47
  878.2 5.6 collective-permute-start
  973.7 3.2 copy-start.1
  980.0 90.4 %all-gather.2.cloned.1.call-start = ((), (), s32[]{:S(2)}) async-start(), calls=%async_computation.2 | async-start | bytes 4259840 | tf_op jit(solution)/shard_map/while/body/eval_jaxpr/all_gather | solution.py:47
  980.2 5.6 collective-permute-start
  1075.7 3.2 copy-start.1
  1082.1 90.4 %all-gather.2.cloned.1.call-start = ((), (), s32[]{:S(2)}) async-start(), calls=%async_computation.2 | async-start | bytes 4259840 | tf_op jit(solution)/shard_map/while/body/eval_jaxpr/all_gather | solution.py:47
  1082.2 5.6 collective-permute-start
  1177.7 3.2 copy-start.1
  1184.1 90.4 %all-gather.2.cloned.1.call-start = ((), (), s32[]{:S(2)}) async-start(), calls=%async_computation.2 | async-start | bytes 4259840 | tf_op jit(solution)/shard_map/while/body/eval_jaxpr/all_gather | solution.py:47
  1184.3 5.6 collective-permute-start
  1279.8 3.2 copy-start.1
  1286.2 0.6 copy-start.2
Sparse Core Ops, SparseCore 0:
  12.7 251.6 reduce-scatter.1
  272.0 84.1 all-gather.1
  374.4 83.8 all-gather.1
  476.4 83.8 all-gather.1
  578.4 83.8 all-gather.1
  680.5 83.8 all-gather.1
  782.5 83.8 all-gather.1
  884.5 83.8 all-gather.1
  986.6 83.8 all-gather.1
  1088.6 83.8 all-gather.1
  1190.7 83.8 all-gather.1
where the time goes:
time: 1290 us
  waiting for transfers between devices  1130 us (88%)
  matrix products  62.5 us (5%)
  local copies, waits for them, and re-layouts  56.1 us (4%)
  starting transfers between devices  19.6 us (2%)
  between operations  13.1 us (1%)
  other arithmetic  13 us (1%)
    all_gather x10, waiting for transfers between devices, advance(): lax.all_gather(reduced, 'tile', axis=2, tiled=True)  840 us
    reduce_scatter x1, waiting for transfers between devices, body(): lax.psum_scatter(dense_sum, 'tile', scatter_dimension=0, tiled=True)  252 us
    all_gather x10, local copies, waits for them, and re-layouts, advance(): lax.all_gather(reduced, 'tile', axis=2, tiled=True)  52.3 us
    ppermute x10, waiting for transfers between devices, shifted(): return lax.ppermute(value, axis, pairs)  35.4 us
    dot_general x10, matrix products, accumulate(): jnp.einsum('jrs,kis->kjri', columns, diag_inverse, precision=highest)  31.3 us
    dot_general x10, matrix products, accumulate(): jnp.einsum('jrs,kis->kjri', columns, coupling, precision=highest)  31.2 us
  transfers between devices with their start and end apart: 21, of which 21 were waited for; matrix products, arithmetic and copies ran while one was open for 0% of the time, Pallas kernels for 0%

commit v1 on v0

--- a/solution.py
+++ b/solution.py
@@ -4,6 +4,16 @@
 from jax.sharding import PartitionSpec as P
 
 highest = lax.Precision.HIGHEST
+
+
+def assign_stages_all(original, array_axis):
+    row_list = []
+    named_axis = "tile"
+    for _ in range(jax.lax.axis_size(named_axis)):
+        row_list.append(original)
+    return jax.lax.all_to_all(
+        jnp.concatenate(row_list, axis=array_axis), named_axis, array_axis, array_axis, tiled=True
+    )
 
 
 def shifted(value, axis, by):
@@ -44,7 +54,7 @@
         active = (batch_index >= 0) & (batch_index < batches)
         clamped = jnp.clip(batch_index, 0, batches - 1)
         reduced = lax.dynamic_index_in_dim(reduced_all, clamped, 0, keepdims=False) - incoming
-        diag_sum, couple_sum = accumulate(lax.all_gather(reduced, "tile", axis=2, tiled=True))
+        diag_sum, couple_sum = accumulate(assign_stages_all(reduced, 2))
         updated = lax.dynamic_update_index_in_dim(solution, combine_parts(diag_sum), clamped, 0)
         return (combine_parts(couple_sum), jnp.where(active, updated, solution))
 

time: 1290 us -> 1060 us (0.82)
  the two profiles are of different devices: /device:TPU:2 before, /device:TPU:16 now
where the time goes in v1:
time: 1060 us
  waiting for transfers between devices  559 us (53%)
  local copies, waits for them, and re-layouts  273 us (26%)
  starting transfers between devices  92.3 us (9%)
  matrix products  78.4 us (7%)
  other arithmetic  38.9 us (4%)
  between operations  13.5 us (1%)
    all_to_all x10, waiting for transfers between devices, assign_stages_all(): jax.lax.all_to_all(jnp.concatenate(row_list, axis=array_axis), named_axis...  299 us
    reduce_scatter x1, waiting for transfers between devices, body(): lax.psum_scatter(dense_sum, 'tile', scatter_dimension=0, tiled=True)  252 us
    while x40, local copies, waits for them, and re-layouts  114 us
    all_to_all x30, local copies, waits for them, and re-layouts, assign_stages_all(): jax.lax.all_to_all(jnp.concatenate(row_list, axis=array_axis), named_axis...  106 us
    all_to_all x10, starting transfers between devices, assign_stages_all(): jax.lax.all_to_all(jnp.concatenate(row_list, axis=array_axis), named_axis...  63.9 us
    concatenate x20, local copies, waits for them, and re-layouts, assign_stages_all(): jnp.concatenate(row_list, axis=array_axis)  50.9 us
    dot_general x10, matrix products, accumulate(): jnp.einsum('jrs,kis->kjri', columns, diag_inverse, precision=highest)  47.2 us
    all_to_all x10, other arithmetic, assign_stages_all(): jax.lax.all_to_all(jnp.concatenate(row_list, axis=array_axis), named_axis...  32.5 us
  transfers between devices with their start and end apart: 21, of which 21 were waited for; matrix products, arithmetic and copies ran while one was open for 0% of the time, Pallas kernels for 0%

profile of v1, /device:TPU:16, one launch (start us, length us, event | category | flops | bytes accessed | tf_op | source)
XLA Modules:
  0.0 1056.4 jit_solution(2679140568349875855)
XLA Ops:
  12.6 251.6 %reduce-scatter.2.cloned.1.call-done = f32[64,192]{1,0:T(8,128)} async-done(((f32[4096,192]{1,0:T(8,128)}), f32[64,192]{1,0:T(8,128)}) %reduce-scatter.2.cloned.1.call-update) | async-done | bytes 49168 | tf_op jit(solution)/shard_map/reduce_scatter | solution.py:39
  265.2 783.8 %while.15 = (s32[]{:T(128)}, f32[2,32,64]{2,1,0:T(8,128)S(1)}, f32[3,2,32,64]{3,2,1,0:T(8,128)S(1)}, s32[]{:T(128)}, f32[3,2,32,64]{3,2,1,0:T(8,128)S(1)}, /*ind...) while((s32[]{:T(128)}, f32[2,32,64]{2,1,0:T(8,128)S(1)}, ...), condition=%wide.region_3.4_spmd, body=%wide.region_2.3_spmd.sunk | while | flops 805330944 | bytes 32915748 | solution.py:62
  272.6 6.5 reshape.130
  279.1 9.2 all-to-all-start
  288.4 28.9 %all-to-all-done = f32[64,1,4096]{2,1,0:T(1,128)S(1)} async-done(((f32[64,1,4096]{2,1,0:T(1,128)}), f32[64,1,4096]{2,1,0:T(1,128)S(1)}, u32[]{:S(2)}, u32[]{:S(2)}) %all-to-all-start) | async-done | bytes 1048608 | tf_op jit(solution)/shard_map/while/body/eval_jaxpr/all_to_all | solution.py:14
  321.1 4.9 reshape.131
  330.6 5.4 copy.55
  336.0 4.7 fusion.41
  354.5 6.5 reshape.130
  361.0 6.1 all-to-all-start
  367.1 28.8 %all-to-all-done = f32[64,1,4096]{2,1,0:T(1,128)S(1)} async-done(((f32[64,1,4096]{2,1,0:T(1,128)}), f32[64,1,4096]{2,1,0:T(1,128)S(1)}, u32[]{:S(2)}, u32[]{:S(2)}) %all-to-all-start) | async-done | bytes 1048608 | tf_op jit(solution)/shard_map/while/body/eval_jaxpr/all_to_all | solution.py:14
  399.7 4.9 reshape.131
  409.3 5.4 copy.55
  414.6 4.7 fusion.41
  422.6 4.9 collective-permute-start
  433.4 6.5 reshape.130
  439.9 5.5 all-to-all-start
  445.5 28.2 %all-to-all-done = f32[64,1,4096]{2,1,0:T(1,128)S(1)} async-done(((f32[64,1,4096]{2,1,0:T(1,128)}), f32[64,1,4096]{2,1,0:T(1,128)S(1)}, u32[]{:S(2)}, u32[]{:S(2)}) %all-to-all-start) | async-done | bytes 1048608 | tf_op jit(solution)/shard_map/while/body/eval_jaxpr/all_to_all | solution.py:14
  477.4 4.9 reshape.131
  487.0 5.4 copy.55
  492.4 4.7 fusion.41
  500.3 5.4 collective-permute-start
  511.6 6.5 reshape.130
  518.1 5.7 all-to-all-start
  523.9 28.9 %all-to-all-done = f32[64,1,4096]{2,1,0:T(1,128)S(1)} async-done(((f32[64,1,4096]{2,1,0:T(1,128)}), f32[64,1,4096]{2,1,0:T(1,128)S(1)}, u32[]{:S(2)}, u32[]{:S(2)}) %all-to-all-start) | async-done | bytes 1048608 | tf_op jit(solution)/shard_map/while/body/eval_jaxpr/all_to_all | solution.py:14
  556.5 4.9 reshape.131
  566.1 5.4 copy.55
  571.5 4.7 fusion.41
  590.0 6.5 reshape.130
  596.5 5.9 all-to-all-start
  602.4 30.6 %all-to-all-done = f32[64,1,4096]{2,1,0:T(1,128)S(1)} async-done(((f32[64,1,4096]{2,1,0:T(1,128)}), f32[64,1,4096]{2,1,0:T(1,128)S(1)}, u32[]{:S(2)}, u32[]{:S(2)}) %all-to-all-start) | async-done | bytes 1048608 | tf_op jit(solution)/shard_map/while/body/eval_jaxpr/all_to_all | solution.py:14
  636.7 4.9 reshape.131
  646.3 5.4 copy.55
  651.7 4.7 fusion.41
  668.2 6.5 reshape.130
  674.7 6.4 all-to-all-start
  681.1 30.7 %all-to-all-done = f32[64,1,4096]{2,1,0:T(1,128)S(1)} async-done(((f32[64,1,4096]{2,1,0:T(1,128)}), f32[64,1,4096]{2,1,0:T(1,128)S(1)}, u32[]{:S(2)}, u32[]{:S(2)}) %all-to-all-start) | async-done | bytes 1048608 | tf_op jit(solution)/shard_map/while/body/eval_jaxpr/all_to_all | solution.py:14
  715.6 4.9 reshape.131
  725.2 5.4 copy.55
  730.6 4.7 fusion.41
  745.8 6.5 reshape.130
  752.3 6.2 all-to-all-start
  758.5 30.9 %all-to-all-done = f32[64,1,4096]{2,1,0:T(1,128)S(1)} async-done(((f32[64,1,4096]{2,1,0:T(1,128)}), f32[64,1,4096]{2,1,0:T(1,128)S(1)}, u32[]{:S(2)}, u32[]{:S(2)}) %all-to-all-start) | async-done | bytes 1048608 | tf_op jit(solution)/shard_map/while/body/eval_jaxpr/all_to_all | solution.py:14
  793.2 4.9 reshape.131
  802.8 5.4 copy.55
  808.1 4.7 fusion.41
  823.3 6.5 reshape.130
  829.8 6.3 all-to-all-start
  836.2 30.9 %all-to-all-done = f32[64,1,4096]{2,1,0:T(1,128)S(1)} async-done(((f32[64,1,4096]{2,1,0:T(1,128)}), f32[64,1,4096]{2,1,0:T(1,128)S(1)}, u32[]{:S(2)}, u32[]{:S(2)}) %all-to-all-start) | async-done | bytes 1048608 | tf_op jit(solution)/shard_map/while/body/eval_jaxpr/all_to_all | solution.py:14
  870.8 4.9 reshape.131
  880.4 5.4 copy.55
  885.8 4.7 fusion.41
  901.0 6.5 reshape.130
  907.5 6.3 all-to-all-start
  913.8 30.9 %all-to-all-done = f32[64,1,4096]{2,1,0:T(1,128)S(1)} async-done(((f32[64,1,4096]{2,1,0:T(1,128)}), f32[64,1,4096]{2,1,0:T(1,128)S(1)}, u32[]{:S(2)}, u32[]{:S(2)}) %all-to-all-start) | async-done | bytes 1048608 | tf_op jit(solution)/shard_map/while/body/eval_jaxpr/all_to_all | solution.py:14
  948.4 4.9 reshape.131
  958.0 5.4 copy.55
  963.4 4.7 fusion.41
  978.6 6.5 reshape.130
  985.1 6.3 all-to-all-start
  991.4 30.9 %all-to-all-done = f32[64,1,4096]{2,1,0:T(1,128)S(1)} async-done(((f32[64,1,4096]{2,1,0:T(1,128)}), f32[64,1,4096]{2,1,0:T(1,128)S(1)}, u32[]{:S(2)}, u32[]{:S(2)}) %all-to-all-start) | async-done | bytes 1048608 | tf_op jit(solution)/shard_map/while/body/eval_jaxpr/all_to_all | solution.py:14
  1026.0 4.9 reshape.131
  1035.6 5.4 copy.55
  1041.0 4.7 fusion.41
  (182 shorter events, 201.8 us)
Async XLA Ops:
  6.5 257.6 %reduce-scatter.2.cloned.1.call-start = ((), (), s32[]{:S(2)}) async-start(), calls=%async_computation.2 | async-start | bytes 4259840 | tf_op jit(solution)/shard_map/reduce_scatter | solution.py:39
  8.3 256.8 %copy-start.2 = (f32[3,2,32,64]{3,2,1,0:T(8,128)S(1)}, f32[3,2,32,64]{3,2,1,0:T(8,128)}, u32[]{:S(2)}) copy-start(f32[3,2,32,64]{3,2,1,0:T(8,128)} %param.8) | copy-start | bytes 147460
  265.4 2.1 collective-permute-start
  279.1 38.2 %all-to-all-start = ((f32[64,1,4096]{2,1,0:T(1,128)}), f32[64,1,4096]{2,1,0:T(1,128)S(1)}, u32[]{:S(2)}, u32[]{:S(2)}) async-start(f32[64,1,4096]{2,1,0:T(1,128)} %reshape.130), calls=%async_computation | async-start | bytes 2097152 | tf_op jit(solution)/shard_map/while/body/eval_jaxpr/all_to_all | solution.py:14
  330.6 10.1 copy-start
  344.0 5.5 collective-permute-start
  361.0 34.8 %all-to-all-start = ((f32[64,1,4096]{2,1,0:T(1,128)}), f32[64,1,4096]{2,1,0:T(1,128)S(1)}, u32[]{:S(2)}, u32[]{:S(2)}) async-start(f32[64,1,4096]{2,1,0:T(1,128)} %reshape.130), calls=%async_computation | async-start | bytes 2097152 | tf_op jit(solution)/shard_map/while/body/eval_jaxpr/all_to_all | solution.py:14
  409.3 10.1 copy-start
  422.6 5.7 collective-permute-start
  439.9 33.7 %all-to-all-start = ((f32[64,1,4096]{2,1,0:T(1,128)}), f32[64,1,4096]{2,1,0:T(1,128)S(1)}, u32[]{:S(2)}, u32[]{:S(2)}) async-start(f32[64,1,4096]{2,1,0:T(1,128)} %reshape.130), calls=%async_computation | async-start | bytes 2097152 | tf_op jit(solution)/shard_map/while/body/eval_jaxpr/all_to_all | solution.py:14
  487.0 10.1 copy-start
  500.3 6.2 collective-permute-start
  518.1 34.6 %all-to-all-start = ((f32[64,1,4096]{2,1,0:T(1,128)}), f32[64,1,4096]{2,1,0:T(1,128)S(1)}, u32[]{:S(2)}, u32[]{:S(2)}) async-start(f32[64,1,4096]{2,1,0:T(1,128)} %reshape.130), calls=%async_computation | async-start | bytes 2097152 | tf_op jit(solution)/shard_map/while/body/eval_jaxpr/all_to_all | solution.py:14
  566.1 10.1 copy-start
  579.5 5.4 collective-permute-start
  596.5 36.5 %all-to-all-start = ((f32[64,1,4096]{2,1,0:T(1,128)}), f32[64,1,4096]{2,1,0:T(1,128)S(1)}, u32[]{:S(2)}, u32[]{:S(2)}) async-start(f32[64,1,4096]{2,1,0:T(1,128)} %reshape.130), calls=%async_computation | async-start | bytes 2097152 | tf_op jit(solution)/shard_map/while/body/eval_jaxpr/all_to_all | solution.py:14
  646.3 10.1 copy-start
  659.7 3.5 collective-permute-start
  674.7 37.1 %all-to-all-start = ((f32[64,1,4096]{2,1,0:T(1,128)}), f32[64,1,4096]{2,1,0:T(1,128)S(1)}, u32[]{:S(2)}, u32[]{:S(2)}) async-start(f32[64,1,4096]{2,1,0:T(1,128)} %reshape.130), calls=%async_computation | async-start | bytes 2097152 | tf_op jit(solution)/shard_map/while/body/eval_jaxpr/all_to_all | solution.py:14
  725.2 10.1 copy-start
  738.5 2.1 collective-permute-start
  752.3 37.1 %all-to-all-start = ((f32[64,1,4096]{2,1,0:T(1,128)}), f32[64,1,4096]{2,1,0:T(1,128)S(1)}, u32[]{:S(2)}, u32[]{:S(2)}) async-start(f32[64,1,4096]{2,1,0:T(1,128)} %reshape.130), calls=%async_computation | async-start | bytes 2097152 | tf_op jit(solution)/shard_map/while/body/eval_jaxpr/all_to_all | solution.py:14
  802.8 10.1 copy-start
  816.1 2.1 collective-permute-start
  829.8 37.2 %all-to-all-start = ((f32[64,1,4096]{2,1,0:T(1,128)}), f32[64,1,4096]{2,1,0:T(1,128)S(1)}, u32[]{:S(2)}, u32[]{:S(2)}) async-start(f32[64,1,4096]{2,1,0:T(1,128)} %reshape.130), calls=%async_computation | async-start | bytes 2097152 | tf_op jit(solution)/shard_map/while/body/eval_jaxpr/all_to_all | solution.py:14
  880.4 10.1 copy-start
  893.7 2.1 collective-permute-start
  907.5 37.2 %all-to-all-start = ((f32[64,1,4096]{2,1,0:T(1,128)}), f32[64,1,4096]{2,1,0:T(1,128)S(1)}, u32[]{:S(2)}, u32[]{:S(2)}) async-start(f32[64,1,4096]{2,1,0:T(1,128)} %reshape.130), calls=%async_computation | async-start | bytes 2097152 | tf_op jit(solution)/shard_map/while/body/eval_jaxpr/all_to_all | solution.py:14
  958.0 10.1 copy-start
  971.3 2.1 collective-permute-start
  985.1 37.2 %all-to-all-start = ((f32[64,1,4096]{2,1,0:T(1,128)}), f32[64,1,4096]{2,1,0:T(1,128)S(1)}, u32[]{:S(2)}, u32[]{:S(2)}) async-start(f32[64,1,4096]{2,1,0:T(1,128)} %reshape.130), calls=%async_computation | async-start | bytes 2097152 | tf_op jit(solution)/shard_map/while/body/eval_jaxpr/all_to_all | solution.py:14
  1035.6 10.1 copy-start
  1049.0 0.6 copy-start.1
Sparse Core Ops, SparseCore 0:
  12.7 251.3 reduce-scatter.1
